TPU v7x, 32 devices: a whole 2x2x4 slice. The times are simulated.
32 devices in a mesh: groups: 1, rows: 2 (over y), chans: 8 (over z, x), cols: 2 (over core).
Axes of the slice: x: 2, y: 2, z: 4, core: 2. Of those that a mesh axis runs over, the one named last changes fastest.
Arguments:
- feature_map: bfloat16 [5, 512, 32, 256], P('groups', 'chans', 'rows', 'cols'), may hold values from -6 to 6
- taps_x: bfloat16 [512, 63], P('chans'), may hold values from -0.75 to 0.75
- taps_y: bfloat16 [512, 63], P('chans'), may hold values from -0.75 to 0.75
- mix_weight: bfloat16 [512, 512], replicated, may hold values from -0.25 to 0.25
- mix_bias: bfloat16 [512], replicated, may hold values from -3 to 3
Outputs:
- section_out: bfloat16 [5, 512, 32, 256], P('groups', 'chans', 'rows', 'cols')
All inputs are finite; a program needn't handle non-finite values.
Results may differ from a plain program's by a relative error of at most 0.0048.
Values may be sent and summed in bfloat16 or wider, within the bound.
A program may use at most 64 MiB of HBM per device.

v0:
```python
import jax
import jax.numpy as jnp
from jax import lax
from jax.sharding import PartitionSpec as P

KERNEL_TAPS = 63
COLUMN_DILATION = 2
ROW_DILATION = 2


def with_halo(block, sides, width):
    for axis, dim in sides:
        count = lax.axis_size(axis)
        forward = [(i, i + 1) for i in range(count - 1)]
        backward = [(target, source) for source, target in forward]
        low = lax.ppermute(
            lax.slice_in_dim(block, block.shape[dim] - width, None, axis=dim), axis, forward
        )
        high = lax.ppermute(lax.slice_in_dim(block, 0, width, axis=dim), axis, backward)
        block = jnp.concatenate([low, block, high], axis=dim)
    return block


def kernel_sweep(border_padded, coefficients, dilation, axis, tally_count):
    array_shape = list(border_padded.shape)
    array_shape[axis] = tally_count
    total = jnp.zeros(tuple(array_shape), jnp.float32)
    for tap in range(coefficients.shape[-1]):
        window = lax.slice_in_dim(
            border_padded, tap * dilation, tap * dilation + tally_count, axis=axis
        )
        total = total + window.astype(jnp.float32) * coefficients[..., tap]
    return total


def rows_pass(tall_rows, kernel):
    row_extent = KERNEL_TAPS // 2 * ROW_DILATION
    coefficients = kernel.astype(jnp.float32)[:, None, None, :]
    border_padded = jnp.pad(tall_rows, ((0, 0), (0, 0), (row_extent, row_extent), (0, 0)))
    return kernel_sweep(border_padded, coefficients, ROW_DILATION, 2, tall_rows.shape[2]).astype(
        jnp.bfloat16
    )


def x_pass(column_widened, taps_x, tally_count):
    column_coefficient = taps_x.astype(jnp.float32)[:, None, None, :]
    return kernel_sweep(column_widened, column_coefficient, COLUMN_DILATION, 3, tally_count).astype(
        jnp.bfloat16
    )


def per_device(feature_map, taps_x, taps_y, mix_weight, mix_bias):
    column_extent = KERNEL_TAPS // 2 * COLUMN_DILATION
    column_widened = with_halo(feature_map, (("cols", 3),), column_extent)
    column_direction = x_pass(column_widened, taps_x, feature_map.shape[3])
    tall_rows = lax.all_to_all(column_direction, "rows", split_axis=1, concat_axis=2, tiled=True)
    per_row = tall_rows.shape[1]
    offset = lax.axis_index("rows") * per_row
    kernel_part = lax.dynamic_slice_in_dim(taps_y, offset, per_row, 0)
    along_tall = rows_pass(tall_rows, kernel_part)
    row_direction = lax.all_to_all(along_tall, "rows", split_axis=2, concat_axis=1, tiled=True)
    spread = lax.all_to_all(row_direction, "chans", split_axis=2, concat_axis=1, tiled=True)
    mixed = jnp.einsum("oc,bchw->bohw", mix_weight, spread, preferred_element_type=jnp.float32)
    bias_full = mix_bias.astype(jnp.float32)[:, None, None]
    activated = jax.nn.gelu(mixed + bias_full, approximate=True).astype(jnp.bfloat16)
    branch = lax.all_to_all(activated, "chans", split_axis=1, concat_axis=2, tiled=True)
    return (feature_map.astype(jnp.float32) + branch.astype(jnp.float32)).astype(jnp.bfloat16)


def solution(mesh):
    return jax.shard_map(
        per_device,
        mesh=mesh,
        in_specs=(
            P("groups", "chans", "rows", "cols"),
            P("chans", None),
            P("chans", None),
            P(),
            P(),
        ),
        out_specs=P("groups", "chans", "rows", "cols"),
        check_vma=False,
    )
```

profile of v0, /device:TPU:0, one launch (start us, length us, event | category | flops | bytes accessed | tf_op | source)
XLA Modules:
  0.0 236.1 jit_solution(4916513972918414027)
XLA Ops:
  0.0 0.0 copy-start
  0.0 3.4 %fusion.113 = (bf16[5,64,16,62]{3,2,1,0:T(8,128)(2,1)}, bf16[5,64,16,62]{3,2,1,0:T(8,128)(2,1)S(1)}) fusion(bf16[5,64,16,128]{3,2,1,0:T(8,128)(2,1)} %param.5), kind=kLoop, calls=%fused_computation.398 | loop fusion | bytes 2539520 | tf_op jit(solution)/shard_map/slice | solution.py:17
  3.4 0.0 copy-start.1
  3.4 3.2 %copy.65 = bf16[5,64,16,62]{1,2,3,0:T(8,128)(2,1)} copy(bf16[5,64,16,62]{3,2,1,0:T(8,128)(2,1)} %get-tuple-element.116) | data formatting | bytes 1269760
  6.7 0.0 copy-start.2
  6.7 3.6 %collective-permute-start = (bf16[5,64,16,62]{1,2,3,0:T(8,128)(2,1)}, bf16[5,64,16,62]{1,2,3,0:T(8,128)(2,1)}, u32[]{:S(2)}, u32[]{:S(2)}) collective-permute-start(bf16[5,64,16,62]{1,2,3,0:T(8,128)(2,1)} %copy.65), channel_id=1, source_target_pairs={{0,1},{2,3},{4,5},{6,7},{8,9},{10,11},{12,13},{14,15},{16,17},{18,... | collective-permute-start | bytes 1904648 | tf_op jit(solution)/shard_map/ppermute | solution.py:16
  10.2 2.1 copy.66
  12.3 1.3 collective-permute-start.1
  13.6 0.0 copy-done.1
  13.6 0.3 copy.39
  14.0 0.0 copy-done.2
  14.0 0.3 slice_reduce_fusion.59
  14.3 0.6 slice_reduce_fusion.62
  14.9 0.6 slice_reduce_fusion.61
  15.6 0.6 slice_reduce_fusion.60
  16.2 0.0 collective-permute-done
  16.2 2.9 %copy.41 = bf16[5,64,16,62]{3,1,2,0:T(8,128)(2,1)} copy(bf16[5,64,16,62]{1,2,3,0:T(8,128)(2,1)} %collective-permute-done) | data formatting | bytes 1269760 | tf_op jit(solution)/shard_map/ppermute | solution.py:16
  19.1 0.0 collective-permute-done.1
  19.1 2.7 %copy.45 = bf16[5,64,16,62]{3,1,2,0:T(8,128)(2,1)} copy(bf16[5,64,16,62]{1,2,3,0:T(8,128)(2,1)} %collective-permute-done.1) | data formatting | bytes 1269760 | tf_op jit(solution)/shard_map/ppermute | solution.py:19
  21.9 76.2 %add_convert_fusion.1 = bf16[5,64,16,128]{3,1,2,0:T(8,128)(2,1)S(1)} fusion(bf16[5,64,16,128]{3,1,2,0:T(8,128)(2,1)S(1)} %copy.39, bf16[5,64,16,62]{3,1,2,0:T(8,128)(2,1)} %copy.45, bf16[5,64,16,62]{3,1,2,0:T(8,128)(2,1)} %copy.41, f32[64]{0:T(128)S(1)} %get-tuple-element.6, f32[64]{0:T(128)S(1)} %get-tuple-element.7, f32[64]{0:T(128)S(1)} %get-tuple-element.8, ...), kind=kLoop, calls=%fused_computation.189 | loop fusion | flops 245760000 | bytes 3907328 | tf_op jit(solution)/shard_map/convert_element_type | solution.py:47
  98.1 0.0 copy-start.3
  98.1 1.9 copy.46
  100.0 3.8 %all-to-all-start = ((bf16[5,64,16,128]{3,2,0,1:T(8,128)(2,1)}), bf16[5,64,16,128]{3,2,0,1:T(8,128)(2,1)S(1)}, u32[]{:S(2)}, u32[]{:S(2)}) async-start(bf16[5,64,16,128]{3,2,0,1:T(8,128)(2,1)} %copy.46), calls=%async_computation | async-start | bytes 2621440 | tf_op jit(solution)/shard_map/all_to_all | solution.py:56
  103.8 0.0 copy-done.3
  103.9 0.3 fusion.109
  104.1 0.6 slice_reduce_fusion.93
  104.7 0.3 fusion.112
  105.0 0.6 slice_reduce_fusion.92
  105.5 14.9 %all-to-all-done = bf16[5,64,16,128]{3,2,0,1:T(8,128)(2,1)S(1)} async-done(((bf16[5,64,16,128]{3,2,0,1:T(8,128)(2,1)}), bf16[5,64,16,128]{3,2,0,1:T(8,128)(2,1)S(1)}, u32[]{:S(2)}, u32[]{:S(2)}) %all-to-all-start) | async-done | bytes 1310752 | tf_op jit(solution)/shard_map/all_to_all | solution.py:56
  120.4 0.2 copy.48
  120.7 9.8 %add_convert_fusion = bf16[5,32,32,128]{3,2,1,0:T(8,128)(2,1)S(1)} fusion(bf16[5,32,32,128]{3,2,1,0:T(8,128)(2,1)S(1)} %bitcast.33, f32[32]{0:T(128)S(1)} %get-tuple-element.101, f32[32]{0:T(128)S(1)} %get-tuple-element.102, f32[32]{0:T(128)S(1)} %get-tuple-element.103, f32[32]{0:T(128)S(1)} %get-tuple-element.104, f32[32]{0:T(128)S(1)} %get-tuple-element.105, ...), kind=kLoop, calls=%fused_computation.188 | loop fusion | flops 72089600 | bytes 2627584 | tf_op jit(solution)/shard_map/convert_element_type | solution.py:40
  130.4 0.5 copy.49
  130.9 20.0 %all_to_all.63 = bf16[5,32,32,128]{3,1,0,2:T(8,128)(2,1)S(1)} all-to-all(bf16[5,32,32,128]{3,1,0,2:T(8,128)(2,1)S(1)} %copy.49), channel_id=1, replica_groups=mesh['groups'=1,'rows'=2,'chans'=8,'cols'=2] {'rows'}, dimensions={2} | all-to-all | bytes 2621440 | tf_op jit(solution)/shard_map/all_to_all | solution.py:61
  150.9 0.5 copy.51
  151.4 0.0 copy-start.4
  151.4 1.4 copy.52
  152.8 6.6 %all-to-all-start.2 = ((bf16[5,64,16,128]{3,1,0,2:T(8,128)(2,1)}), bf16[5,64,16,128]{3,1,0,2:T(8,128)(2,1)S(1)}, u32[]{:S(2)}, u32[]{:S(2)}) async-start(bf16[5,64,16,128]{3,1,0,2:T(8,128)(2,1)} %copy.52), calls=%async_computation.2 | async-start | bytes 2621440 | tf_op jit(solution)/shard_map/all_to_all | solution.py:62
  159.5 0.0 copy-done.4
  159.5 31.6 %all-to-all-done.2 = bf16[5,64,16,128]{3,1,0,2:T(8,128)(2,1)S(1)} async-done(((bf16[5,64,16,128]{3,1,0,2:T(8,128)(2,1)}), bf16[5,64,16,128]{3,1,0,2:T(8,128)(2,1)S(1)}, u32[]{:S(2)}, u32[]{:S(2)}) %all-to-all-start.2) | async-done | bytes 1310752 | tf_op jit(solution)/shard_map/all_to_all | solution.py:62
  191.2 0.1 copy.54
  191.3 0.0 copy-done
  191.3 2.6 %fusion.33 = bf16[5,512,2,128]{1,3,2,0:T(8,128)(2,1)} fusion(bf16[5,512,2,128]{3,1,2,0:T(8,128)(2,1)S(1)} %bitcast.38, f32[512]{0:T(512)S(1)} %convert_element_type.474, bf16[512,512]{1,0:T(8,128)(2,1)S(1)} %copy-done), kind=kOutput, calls=%fused_computation.186 | convolution fusion | flops 677642240 | bytes 3147776 | tf_op jit(solution)/shard_map/oc,bchw->bohw/dot_general | solution.py:63
  193.9 3.9 %copy.56 = bf16[5,512,2,128]{3,2,0,1:T(2,128)(2,1)S(1)} copy(bf16[5,512,2,128]{1,3,2,0:T(8,128)(2,1)} %fusion.33) | data formatting | bytes 2621440 | tf_op jit(solution)/shard_map/convert_element_type | solution.py:65
  197.8 35.0 %all_to_all.64 = bf16[5,512,2,128]{3,2,0,1:T(2,128)(2,1)S(1)} all-to-all(bf16[5,512,2,128]{3,2,0,1:T(2,128)(2,1)S(1)} %copy.56), channel_id=1, replica_groups=mesh['groups'=1,'rows'=2,'chans'=8,'cols'=2] {'chans'}, dimensions={1} | all-to-all | bytes 2621440 | tf_op jit(solution)/shard_map/all_to_all | solution.py:66
  232.8 0.2 copy.57
  233.0 0.3 convert_bitcast_fusion
  233.3 0.3 copy.58
  233.6 0.6 fusion.25
  234.2 1.9 copy.59
  (3 shorter events, 0.0 us)
Async XLA Ops:
  0.0 191.3 %copy-start = (bf16[512,512]{1,0:T(8,128)(2,1)S(1)}, bf16[512,512]{1,0:T(8,128)(2,1)}, u32[]{:S(2)}) copy-start(bf16[512,512]{1,0:T(8,128)(2,1)} %param.8) | copy-start | bytes 1572868
  3.4 10.2 %copy-start.1 = (bf16[5,64,16,128]{3,2,1,0:T(8,128)(2,1)S(1)}, bf16[5,64,16,128]{3,2,1,0:T(8,128)(2,1)}, u32[]{:S(2)}) copy-start(bf16[5,64,16,128]{3,2,1,0:T(8,128)(2,1)} %param.5) | copy-start | bytes 3932164
  6.7 7.3 %copy-start.2 = (bf16[64,63]{1,0:T(8,128)(2,1)S(1)}, bf16[64,63]{1,0:T(8,128)(2,1)}, u32[]{:S(2)}) copy-start(bf16[64,63]{1,0:T(8,128)(2,1)} %param.6) | copy-start | bytes 24196
  6.7 9.5 %collective-permute-start = (bf16[5,64,16,62]{1,2,3,0:T(8,128)(2,1)}, bf16[5,64,16,62]{1,2,3,0:T(8,128)(2,1)}, u32[]{:S(2)}, u32[]{:S(2)}) collective-permute-start(bf16[5,64,16,62]{1,2,3,0:T(8,128)(2,1)} %copy.65), channel_id=1, source_target_pairs={{0,1},{2,3},{4,5},{6,7},{8,9},{10,11},{12,13},{14,15},{16,17},{18,... | collective-permute-start | bytes 1904648 | tf_op jit(solution)/shard_map/ppermute | solution.py:16
  12.3 6.8 %collective-permute-start.1 = (bf16[5,64,16,62]{1,2,3,0:T(8,128)(2,1)}, bf16[5,64,16,62]{1,2,3,0:T(8,128)(2,1)}, u32[]{:S(2)}, u32[]{:S(2)}) collective-permute-start(bf16[5,64,16,62]{1,2,3,0:T(8,128)(2,1)} %copy.66), channel_id=1, source_target_pairs={{1,0},{3,2},{5,4},{7,6},{9,8},{11,10},{13,12},{15,14},{17,16},{19,... | collective-permute-start | bytes 1904648 | tf_op jit(solution)/shard_map/ppermute | solution.py:19
  98.1 5.8 %copy-start.3 = (bf16[64,63]{1,0:T(8,128)(2,1)S(1)}, bf16[64,63]{1,0:T(8,128)(2,1)}, u32[]{:S(2)}) copy-start(bf16[64,63]{1,0:T(8,128)(2,1)} %param.7) | copy-start | bytes 24196
  100.0 20.4 %all-to-all-start = ((bf16[5,64,16,128]{3,2,0,1:T(8,128)(2,1)}), bf16[5,64,16,128]{3,2,0,1:T(8,128)(2,1)S(1)}, u32[]{:S(2)}, u32[]{:S(2)}) async-start(bf16[5,64,16,128]{3,2,0,1:T(8,128)(2,1)} %copy.46), calls=%async_computation | async-start | bytes 2621440 | tf_op jit(solution)/shard_map/all_to_all | solution.py:56
  151.4 8.1 %copy-start.4 = (bf16[512]{0:T(512)(128)(2,1)S(1)}, bf16[512]{0:T(512)(128)(2,1)}, u32[]{:S(2)}) copy-start(bf16[512]{0:T(512)(128)(2,1)} %param.9) | copy-start | bytes 3076
  152.8 38.3 %all-to-all-start.2 = ((bf16[5,64,16,128]{3,1,0,2:T(8,128)(2,1)}), bf16[5,64,16,128]{3,1,0,2:T(8,128)(2,1)S(1)}, u32[]{:S(2)}, u32[]{:S(2)}) async-start(bf16[5,64,16,128]{3,1,0,2:T(8,128)(2,1)} %copy.52), calls=%async_computation.2 | async-start | bytes 2621440 | tf_op jit(solution)/shard_map/all_to_all | solution.py:62
where the time goes:
time: 237 us; the launch traced here: 236 us
  other arithmetic  88 us (37%)
  blocking collectives  54.9 us (23%)
  waiting for transfers between devices  46.5 us (20%)
  local copies, waits for them, and re-layouts  28.5 us (12%)
  starting transfers between devices  15.3 us (6%)
  matrix products  2.62 us (1%)
    convert_element_type x1, other arithmetic, x_pass(): kernel_sweep(column_widened, column_coefficient, COLUMN_DILATION, 3, tall...  76.2 us
    all_to_all x1, blocking collectives, per_device(): lax.all_to_all(activated, 'chans', split_axis=1, concat_axis=2, tiled=True)  35 us
    all_to_all x1, waiting for transfers between devices, per_device(): lax.all_to_all(row_direction, 'chans', split_axis=2, concat_axis=1, tiled...  31.6 us
    all_to_all x1, blocking collectives, per_device(): lax.all_to_all(along_tall, 'rows', split_axis=2, concat_axis=1, tiled=True)  20 us
    all_to_all x1, waiting for transfers between devices, per_device(): lax.all_to_all(column_direction, 'rows', split_axis=1, concat_axis=2, til...  14.9 us
    convert_element_type x1, other arithmetic, rows_pass(): kernel_sweep(border_padded, coefficients, ROW_DILATION, 2, tall_rows.shap...  9.77 us
    all_to_all x1, starting transfers between devices, per_device(): lax.all_to_all(row_direction, 'chans', split_axis=2, concat_axis=1, tiled...  6.63 us
    unnamed x13, local copies, waits for them, and re-layouts  5.71 us
  transfers between devices with their start and end apart: 4, of which 2 were waited for; matrix products, arithmetic and copies ran while one was open for 4% of the time, Pallas kernels for 0%

commit v1 on v0

--- a/solution.py
+++ b/solution.py
@@ -1,11 +1,19 @@
+import functools
+
 import jax
 import jax.numpy as jnp
 from jax import lax
+from jax.experimental import pallas as pl
+from jax.experimental.pallas import tpu as pltpu
 from jax.sharding import PartitionSpec as P
 
 KERNEL_TAPS = 63
+HALF = KERNEL_TAPS // 2
 COLUMN_DILATION = 2
 ROW_DILATION = 2
+MESH = pl.DeviceIdType.MESH
+BF16 = jnp.bfloat16
+F32 = jnp.float32
 
 
 def with_halo(block, sides, width):
@@ -49,7 +57,7 @@
     )
 
 
-def per_device(feature_map, taps_x, taps_y, mix_weight, mix_bias):
+def per_device_general(feature_map, taps_x, taps_y, mix_weight, mix_bias):
     column_extent = KERNEL_TAPS // 2 * COLUMN_DILATION
     column_widened = with_halo(feature_map, (("cols", 3),), column_extent)
     column_direction = x_pass(column_widened, taps_x, feature_map.shape[3])
@@ -67,9 +75,279 @@
     return (feature_map.astype(jnp.float32) + branch.astype(jnp.float32)).astype(jnp.bfloat16)
 
 
+def dot(a, b):
+    return jnp.dot(a, b, preferred_element_type=F32)
+
+
+def iota(shape, dim):
+    return lax.broadcasted_iota(jnp.int32, shape, dim)
+
+
+def section_kernel(
+    dims,
+    feat_hbm, tapx_ref, tapy_ref, weight_ref, bias_ref,
+    out_ref,
+    feat, whole, toep, rowmat, swap, biasb, xbuf, ybuf, gath, brch, back,
+    loc_sem, asend, arecv, csend, crecv, dsend, drecv,
+):
+    T, nr, nch, nco, C, CB, H, W = dims
+    quads = nr * nco
+    cq = CB // quads
+    FH, FW = nr * H, nco * W
+    rp = H // nch
+    r, ch, co = lax.axis_index("rows"), lax.axis_index("chans"), lax.axis_index("cols")
+    q = r * nco + co
+
+    def peer(dr, i, dc):
+        return lax.rem(r + dr, nr), lax.rem(ch + i, nch), lax.rem(co + dc, nco)
+
+    def dev(p):
+        return {"rows": p[0], "chans": p[1], "cols": p[2]}
+
+    barrier = pltpu.get_barrier_semaphore()
+
+    def greet(i, skip_self):
+        for dr in range(nr):
+            for dc in range(nco):
+                if skip_self and dr == 0 and dc == 0:
+                    continue
+                pl.semaphore_signal(
+                    barrier, inc=1, device_id=dev(peer(dr, i, dc)), device_id_type=MESH
+                )
+
+    greet(0, True)
+
+    @pl.loop(1, nch)
+    def _(i):
+        greet(i, False)
+
+    own = pltpu.make_async_copy(feat_hbm, feat, loc_sem.at[0])
+    own.start()
+    mine = []
+    for t in range(T):
+        c = pltpu.make_async_copy(
+            feat_hbm.at[t, pl.ds(pl.multiple_of(q * cq, cq), cq)],
+            whole.at[t, :, pl.ds(pl.multiple_of(r * H, H), H), pl.ds(pl.multiple_of(co * W, W), W)],
+            loc_sem.at[1 + t],
+        )
+        c.start()
+        mine.append(c)
+
+    pl.semaphore_wait(barrier, nr * nch * nco - 1)
+
+    for t in range(T):
+        for dr in range(nr):
+            for dc in range(nco):
+                if dr == 0 and dc == 0:
+                    continue
+                p = peer(dr, 0, dc)
+                pq = p[0] * nco + p[2]
+                pltpu.make_async_remote_copy(
+                    src_ref=feat_hbm.at[t, pl.ds(pl.multiple_of(pq * cq, cq), cq)],
+                    dst_ref=whole.at[
+                        t, :, pl.ds(pl.multiple_of(r * H, H), H), pl.ds(pl.multiple_of(co * W, W), W)
+                    ],
+                    send_sem=asend,
+                    recv_sem=arecv.at[t],
+                    device_id=dev(p),
+                    device_id_type=MESH,
+                ).start()
+
+    qs = pl.ds(pl.multiple_of(q * cq, cq), cq)
+    tx = tapx_ref[qs, :]
+    ty = tapy_ref[qs, :]
+    tap = iota((KERNEL_TAPS, FW), 0)
+    pos = iota((KERNEL_TAPS, FW), 1)
+    d = lax.rem(HALF * COLUMN_DILATION - COLUMN_DILATION * tap + FW, FW)
+    spread_x = dot(tx, (pos == d).astype(F32).astype(BF16))
+    jj = iota((16, FW), 0)
+    ww = iota((16, FW), 1)
+    reach = HALF * COLUMN_DILATION
+    for c in range(cq):
+        base = jnp.broadcast_to(spread_x[c : c + 1, :], (16, FW))
+        base = pltpu.roll(base, 0, 1, stride=1, stride_axis=0)
+        for b in range(FW // 16):
+            rolled = base if b == 0 else pltpu.roll(base, 16 * b, 1)
+            delta = ww - jj - 16 * b
+            keep = (delta <= reach) & (delta >= -reach)
+            toep[c, pl.ds(16 * b, 16), :] = jnp.where(keep, rolled, 0.0).astype(BF16)
+
+    KK = cq * FH
+    tap = iota((KERNEL_TAPS, FH), 0)
+    pos = iota((KERNEL_TAPS, FH), 1)
+    own_channel = (iota((cq, KK), 1) // FH) == iota((cq, KK), 0)
+    for h in range(FH):
+        pick = (pos - h) == ROW_DILATION * (tap - HALF)
+        one = dot(ty, pick.astype(F32).astype(BF16))
+        tiled = jnp.concatenate([one] * cq, axis=1)
+        rowmat[pl.ds(h * cq, cq), :] = jnp.where(own_channel, tiled, 0.0).astype(BF16)
+
+    a = iota((16 * H, 16 * H), 0)
+    b = iota((16 * H, 16 * H), 1)
+    swap[...] = ((a // H == lax.rem(b, 16)) & (lax.rem(a, H) == b // 16)).astype(F32).astype(BF16)
+    diag = jnp.where(
+        iota((C, C), 0) == iota((C, C), 1), jnp.broadcast_to(bias_ref[...].astype(F32), (C, C)), 0.0
+    )
+    biasb[...] = dot(diag.astype(BF16), jnp.ones((C, W), BF16))
+
+    for c in mine:
+        c.wait()
+    own.wait()
+
+    block = ch * quads + q
+    chan_rows = pl.ds(pl.multiple_of(block * cq, cq), cq)
+
+    def conv(t):
+        landed = whole.at[0, pl.ds(0, cq // quads * (quads - 1))]
+        pltpu.make_async_copy(landed, landed, arecv.at[t]).wait()
+
+        @pl.loop(0, cq)
+        def _(c):
+            xbuf[pl.ds(pl.multiple_of(c * FH, FH), FH), :] = dot(whole[t, c], toep[c]).astype(BF16)
+
+        along = dot(rowmat[...], xbuf[...]).astype(BF16).reshape(FH, cq, FW)
+        for k in range(nco):
+            ybuf[t, k] = along[:, :, k * W : (k + 1) * W]
+
+        def piece(p):
+            return ybuf.at[t, p[2], pl.ds(p[0] * H + p[1] * rp, rp)]
+
+        def push(i, dr, dc):
+            p = peer(dr, i, dc)
+            pltpu.make_async_remote_copy(
+                src_ref=piece(p),
+                dst_ref=gath.at[t, :, chan_rows, :],
+                send_sem=csend,
+                recv_sem=crecv.at[t],
+                device_id=dev(p),
+                device_id_type=MESH,
+            ).start()
+
+        @pl.loop(0, nch - 1)
+        def _(s):
+            i = lax.rem(s + nch // 2 - 1, nch - 1) + 1
+            for dr in range(nr):
+                for dc in range(nco):
+                    push(i, dr, dc)
+
+        for dr in range(nr):
+            for dc in range(nco):
+                if dr or dc:
+                    push(0, dr, dc)
+        pltpu.make_async_copy(
+            piece((r, ch, co)), gath.at[t, :, chan_rows, :], crecv.at[t]
+        ).start()
+
+    def mix(t):
+        pltpu.make_async_copy(gath.at[t], gath.at[t], crecv.at[t]).wait()
+        for k in range(rp):
+            v = dot(weight_ref[...], gath[t, k]) + biasb[...]
+            inner = 0.7978845608028654 * (v + 0.044715 * (v * v * v))
+            brch[t, k] = (0.5 * v * (1.0 + jnp.tanh(inner))).astype(BF16)
+
+        def piece(pc):
+            return brch.at[t, :, pl.ds(pl.multiple_of(pc * CB, CB), CB), :]
+
+        spot = pl.ds(ch * rp, rp)
+
+        @pl.loop(0, nch - 1)
+        def _(s):
+            i = lax.rem(s + nch // 2 - 1, nch - 1) + 1
+            p = peer(0, i, 0)
+            pltpu.make_async_remote_copy(
+                src_ref=piece(p[1]),
+                dst_ref=back.at[t, spot],
+                send_sem=dsend,
+                recv_sem=drecv.at[t],
+                device_id=dev(p),
+                device_id_type=MESH,
+            ).start()
+
+        pltpu.make_async_copy(piece(ch), back.at[t, spot], drecv.at[t]).start()
+
+    def finish(t):
+        pltpu.make_async_copy(back.at[t], back.at[t], drecv.at[t]).wait()
+        for g in range(CB // 16):
+            rows = back[t, :, g * 16 : (g + 1) * 16, :].reshape(H * 16, W)
+            branch = dot(swap[...], rows).reshape(16, H, W)
+            out_ref[t, g * 16 : (g + 1) * 16] = (
+                feat[t, g * 16 : (g + 1) * 16].astype(F32) + branch
+            ).astype(BF16)
+
+    lag1, lag2 = 2, 4
+
+    @pl.loop(0, T + lag2)
+    def _(s):
+        @pl.when(s < T)
+        def _():
+            conv(s)
+
+        @pl.when((s >= lag1) & (s < T + lag1))
+        def _():
+            mix(s - lag1)
+
+        @pl.when(s >= lag2)
+        def _():
+            finish(s - lag2)
+
+    sent = whole.at[:, pl.ds(0, cq // quads * (quads - 1))]
+    pltpu.make_async_copy(sent, sent, asend).wait()
+    parts = nr * nch * nco
+    sent = gath.at[:, :, pl.ds(0, C // parts * (parts - 1)), :]
+    pltpu.make_async_copy(sent, sent, csend).wait()
+    sent = brch.at[:, :, pl.ds(0, C // nch * (nch - 1)), :]
+    pltpu.make_async_copy(sent, sent, dsend).wait()
+
+
+def per_device(mesh, feature_map, taps_x, taps_y, mix_weight, mix_bias):
+    T, CB, H, W = feature_map.shape
+    C = mix_weight.shape[0]
+    nr, nch, nco = (mesh.shape[a] for a in ("rows", "chans", "cols"))
+    quads = nr * nco
+    cq = CB // quads
+    rp = H // max(nch, 1)
+    FH, FW = nr * H, nco * W
+    dims = (T, nr, nch, nco, C, CB, H, W)
+    return pl.pallas_call(
+        functools.partial(section_kernel, dims),
+        out_shape=jax.ShapeDtypeStruct(feature_map.shape, BF16),
+        in_specs=[pl.BlockSpec(memory_space=pl.ANY)]
+        + [pl.BlockSpec(memory_space=pltpu.VMEM)] * 4,
+        out_specs=pl.BlockSpec(memory_space=pltpu.VMEM),
+        scratch_shapes=[
+            pltpu.VMEM((T, CB, H, W), BF16),
+            pltpu.VMEM((T, cq, FH, FW), BF16),
+            pltpu.VMEM((cq, FW, FW), BF16),
+            pltpu.VMEM((FH * cq, cq * FH), BF16),
+            pltpu.VMEM((16 * H, 16 * H), BF16),
+            pltpu.VMEM((C, W), F32),
+            pltpu.VMEM((cq * FH, FW), BF16),
+            pltpu.VMEM((T, nco, FH, cq, W), BF16),
+            pltpu.VMEM((T, rp, C, W), BF16),
+            pltpu.VMEM((T, rp, C, W), BF16),
+            pltpu.VMEM((T, H, CB, W), BF16),
+            pltpu.SemaphoreType.DMA((1 + T,)),
+            pltpu.SemaphoreType.DMA,
+            pltpu.SemaphoreType.DMA((T,)),
+            pltpu.SemaphoreType.DMA,
+            pltpu.SemaphoreType.DMA((T,)),
+            pltpu.SemaphoreType.DMA,
+            pltpu.SemaphoreType.DMA((T,)),
+        ],
+        compiler_params=pltpu.CompilerParams(
+            collective_id=0, has_side_effects=True, vmem_limit_bytes=40 * 1024 * 1024
+        ),
+    )(feature_map, taps_x, taps_y, mix_weight, mix_bias.reshape(1, C))
+
+
+def fits_kernel(mesh):
+    return mesh.shape["rows"] == 2 and mesh.shape["cols"] == 2 and mesh.shape["chans"] == 8
+
+
 def solution(mesh):
+    body = functools.partial(per_device, mesh) if fits_kernel(mesh) else per_device_general
     return jax.shard_map(
-        per_device,
+        body,
         mesh=mesh,
         in_specs=(
             P("groups", "chans", "rows", "cols"),

time: 237 us -> 78.3 us (0.33)
  other arithmetic: 88 us -> 0 us
  Pallas kernels: 0 us -> 72.4 us
  blocking collectives: 54.9 us -> 0 us
  waiting for transfers between devices: 46.5 us -> 0 us
  local copies, waits for them, and re-layouts: 28.5 us -> 5.53 us
  starting transfers between devices: 15.3 us -> 0 us
  matrix products: 2.62 us -> 0 us
    convert_element_type x5 -> x0, other arithmetic: 86.8 us -> none  [the longest x1 76.2 us: x_pass(): kernel_sweep(column_widened, column_coefficient, COLUMN_DILATION, 3, tall...]
    pallas_call x0 -> x1, Pallas kernels: none -> 72.4 us  [per_device(): pl.pallas_call(functools.partial(section_kernel, dims), out_shape=jax.Sha...]
    all_to_all x2 -> x0, blocking collectives: 54.9 us -> none  [the longest x1 35 us: per_device(): lax.all_to_all(activated, 'chans', split_axis=1, concat_axis=2, tiled=True)]
    all_to_all x2 -> x0, waiting for transfers between devices: 46.5 us -> none  [the longest x1 31.6 us: per_device(): lax.all_to_all(row_direction, 'chans', split_axis=2, concat_axis=1, tiled...]
    all_to_all x2 -> x0, starting transfers between devices: 10.5 us -> none  [the longest x1 6.63 us: per_device(): lax.all_to_all(row_direction, 'chans', split_axis=2, concat_axis=1, tiled...]
    convert_element_type x5 -> x0, local copies, waits for them, and re-layouts: 8.52 us -> none  [the longest x1 3.89 us: per_device(): jax.nn.gelu(mixed + bias_full, approximate=True).astype(jnp.bfloat16)]
    slice x6 -> x0, local copies, waits for them, and re-layouts: 6.16 us -> none  [the longest x1 3.43 us: with_halo(): lax.slice_in_dim(block, block.shape[dim] - width, None, axis=dim)]
    ppermute x2 -> x0, local copies, waits for them, and re-layouts: 5.66 us -> none  [the longest x1 2.93 us: with_halo(): lax.ppermute(lax.slice_in_dim(block, block.shape[dim] - width, None, axis...]
  transfers between devices with their start and end apart: 4 -> 0, of which waited for: 2 -> 0; matrix products, arithmetic and copies ran while one was open for 4% -> 0% of each run, Pallas kernels for 0% -> 0%
where the time goes in v1:
time: 78.3 us; the launch traced here: 77.9 us
  Pallas kernels  72.4 us (92%)
  local copies, waits for them, and re-layouts  5.53 us (7%)
    pallas_call x1, Pallas kernels, per_device(): pl.pallas_call(functools.partial(section_kernel, dims), out_shape=jax.Sha...  72.4 us
    unnamed x9, local copies, waits for them, and re-layouts  4.85 us

profile of v1, /device:TPU:0, one launch (start us, length us, event | category | flops | bytes accessed | tf_op | source)
XLA Modules:
  0.0 77.9 jit_solution(14992712958772671852)
XLA Ops:
  0.0 0.7 reshape.3.bias_ref
  0.7 0.0 copy-start
  0.7 1.3 %copy-done = bf16[5,64,16,128]{3,2,1,0:T(8,128)(2,1)S(1)} copy-done((bf16[5,64,16,128]{3,2,1,0:T(8,128)(2,1)S(1)}, bf16[5,64,16,128]{3,2,1,0:T(8,128)(2,1)}, u32[]{:S(2)}) %copy-start) | copy-done | bytes 1310744
  2.0 0.0 copy-start.1
  2.0 1.0 %copy-done.1 = bf16[512,512]{1,0:T(8,128)(2,1)S(1)} copy-done((bf16[512,512]{1,0:T(8,128)(2,1)S(1)}, bf16[512,512]{1,0:T(8,128)(2,1)}, u32[]{:S(2)}) %copy-start.1) | copy-done | bytes 524312
  3.0 0.0 copy-start.2
  3.0 0.7 copy-done.2
  3.8 0.0 copy-start.3
  3.8 0.7 copy-done.3
  4.5 72.4 %shard_map.55 = bf16[5,64,16,128]{3,2,1,0:T(8,128)(2,1)S(1)} custom-call(bf16[5,64,16,128]{3,2,1,0:T(8,128)(2,1)S(1)} %copy-done, bf16[64,63]{1,0:T(8,128)(2,1)S(1)} %copy-done.2, bf16[64,63]{1,0:T(8,128)(2,1)S(1)} %copy-done.3, bf16[512,512]{1,0:T(8,128)(2,1)S(1)} %copy-done.1, bf16[1,512]{1,0:T(2,128)(2,1)S(1)} %reshape.3.bias_ref), custom_call_target="tpu_custom_call" | custom-call | tf_op jit(solution)/shard_map/pallas_call | solution.py:311
  76.8 1.1 %copy.7 = bf16[5,64,16,128]{3,2,1,0:T(8,128)(2,1)} copy(bf16[5,64,16,128]{3,2,1,0:T(8,128)(2,1)S(1)} %shard_map.55) | data formatting | bytes 2621440
Async XLA Ops:
  0.7 1.3 %copy-start = (bf16[5,64,16,128]{3,2,1,0:T(8,128)(2,1)S(1)}, bf16[5,64,16,128]{3,2,1,0:T(8,128)(2,1)}, u32[]{:S(2)}) copy-start(bf16[5,64,16,128]{3,2,1,0:T(8,128)(2,1)} %feat_hbm.1) | copy-start | bytes 3932164
  2.0 1.0 %copy-start.1 = (bf16[512,512]{1,0:T(8,128)(2,1)S(1)}, bf16[512,512]{1,0:T(8,128)(2,1)}, u32[]{:S(2)}) copy-start(bf16[512,512]{1,0:T(8,128)(2,1)} %weight_ref.1) | copy-start | bytes 1572868
  3.0 0.7 copy-start.2
  3.8 0.7 copy-start.3

commit v2 on v1

--- a/solution.py
+++ b/solution.py
@@ -85,8 +85,9 @@
 
 def section_kernel(
     dims,
-    feat_hbm, tapx_ref, tapy_ref, weight_ref, bias_ref,
+    feat_hbm, tapx_hbm, tapy_hbm, weight_hbm, bias_hbm,
     out_ref,
+    tapx_ref, tapy_ref, weight_ref, bias_ref,
     feat, whole, toep, rowmat, swap, biasb, xbuf, ybuf, gath, brch, back,
     loc_sem, asend, arecv, csend, crecv, dsend, drecv,
 ):
@@ -121,13 +122,19 @@
     def _(i):
         greet(i, False)
 
+    small = []
+    for k, (src, dst) in enumerate(
+        ((tapx_hbm, tapx_ref), (tapy_hbm, tapy_ref), (bias_hbm, bias_ref), (weight_hbm, weight_ref))
+    ):
+        c = pltpu.make_async_copy(src, dst, loc_sem.at[1 + T + k])
+        c.start()
+        small.append(c)
     own = pltpu.make_async_copy(feat_hbm, feat, loc_sem.at[0])
-    own.start()
     mine = []
     for t in range(T):
         c = pltpu.make_async_copy(
             feat_hbm.at[t, pl.ds(pl.multiple_of(q * cq, cq), cq)],
-            whole.at[t, :, pl.ds(pl.multiple_of(r * H, H), H), pl.ds(pl.multiple_of(co * W, W), W)],
+            whole.at[t, r, co],
             loc_sem.at[1 + t],
         )
         c.start()
@@ -135,24 +142,32 @@
 
     pl.semaphore_wait(barrier, nr * nch * nco - 1)
 
-    for t in range(T):
-        for dr in range(nr):
+    cs = cq // nch
+
+    def share(t, first, count):
+        for dr in range(nr - 1, -1, -1):
             for dc in range(nco):
                 if dr == 0 and dc == 0:
                     continue
                 p = peer(dr, 0, dc)
                 pq = p[0] * nco + p[2]
                 pltpu.make_async_remote_copy(
-                    src_ref=feat_hbm.at[t, pl.ds(pl.multiple_of(pq * cq, cq), cq)],
-                    dst_ref=whole.at[
-                        t, :, pl.ds(pl.multiple_of(r * H, H), H), pl.ds(pl.multiple_of(co * W, W), W)
-                    ],
+                    src_ref=feat_hbm.at[t, pl.ds(pq * cq + first, count)],
+                    dst_ref=whole.at[t, r, co, pl.ds(first, count)],
                     send_sem=asend,
                     recv_sem=arecv.at[t],
                     device_id=dev(p),
                     device_id_type=MESH,
                 ).start()
 
+    ahead = 2
+    for t in range(min(ahead, T)):
+        share(t, 0, cq)
+
+    own.start()
+
+    for c in small:
+        c.wait()
     qs = pl.ds(pl.multiple_of(q * cq, cq), cq)
     tx = tapx_ref[qs, :]
     ty = tapy_ref[qs, :]
@@ -186,7 +201,7 @@
     b = iota((16 * H, 16 * H), 1)
     swap[...] = ((a // H == lax.rem(b, 16)) & (lax.rem(a, H) == b // 16)).astype(F32).astype(BF16)
     diag = jnp.where(
-        iota((C, C), 0) == iota((C, C), 1), jnp.broadcast_to(bias_ref[...].astype(F32), (C, C)), 0.0
+        iota((C, C), 0) == iota((C, C), 1), jnp.broadcast_to(bias_ref[...].astype(F32).reshape(1, C), (C, C)), 0.0
     )
     biasb[...] = dot(diag.astype(BF16), jnp.ones((C, W), BF16))
 
@@ -197,13 +212,19 @@
     block = ch * quads + q
     chan_rows = pl.ds(pl.multiple_of(block * cq, cq), cq)
 
+    def full_map(t, c):
+        bands = [
+            jnp.concatenate([whole[t, i, j, c] for j in range(nco)], axis=1) for i in range(nr)
+        ]
+        return jnp.concatenate(bands, axis=0)
+
     def conv(t):
-        landed = whole.at[0, pl.ds(0, cq // quads * (quads - 1))]
+        landed = whole.at[0, :, :, pl.ds(0, cq // quads * (quads - 1))]
         pltpu.make_async_copy(landed, landed, arecv.at[t]).wait()
 
-        @pl.loop(0, cq)
+        @pl.loop(0, cq, unroll=4)
         def _(c):
-            xbuf[pl.ds(pl.multiple_of(c * FH, FH), FH), :] = dot(whole[t, c], toep[c]).astype(BF16)
+            xbuf[pl.ds(pl.multiple_of(c * FH, FH), FH), :] = dot(full_map(t, c), toep[c]).astype(BF16)
 
         along = dot(rowmat[...], xbuf[...]).astype(BF16).reshape(FH, cq, FW)
         for k in range(nco):
@@ -225,10 +246,18 @@
 
         @pl.loop(0, nch - 1)
         def _(s):
-            i = lax.rem(s + nch // 2 - 1, nch - 1) + 1
+            @pl.when(t + ahead < T)
+            def _():
+                share(t + ahead, s * cs, cs)
+
+            i = s + 1
             for dr in range(nr):
                 for dc in range(nco):
                     push(i, dr, dc)
+
+        @pl.when(t + ahead < T)
+        def _():
+            share(t + ahead, (nch - 1) * cs, cs)
 
         for dr in range(nr):
             for dc in range(nco):
@@ -252,7 +281,7 @@
 
         @pl.loop(0, nch - 1)
         def _(s):
-            i = lax.rem(s + nch // 2 - 1, nch - 1) + 1
+            i = s + 1
             p = peer(0, i, 0)
             pltpu.make_async_remote_copy(
                 src_ref=piece(p[1]),
@@ -290,7 +319,7 @@
         def _():
             finish(s - lag2)
 
-    sent = whole.at[:, pl.ds(0, cq // quads * (quads - 1))]
+    sent = whole.at[:, :, :, pl.ds(0, cq // quads * (quads - 1))]
     pltpu.make_async_copy(sent, sent, asend).wait()
     parts = nr * nch * nco
     sent = gath.at[:, :, pl.ds(0, C // parts * (parts - 1)), :]
@@ -311,12 +340,15 @@
     return pl.pallas_call(
         functools.partial(section_kernel, dims),
         out_shape=jax.ShapeDtypeStruct(feature_map.shape, BF16),
-        in_specs=[pl.BlockSpec(memory_space=pl.ANY)]
-        + [pl.BlockSpec(memory_space=pltpu.VMEM)] * 4,
+        in_specs=[pl.BlockSpec(memory_space=pltpu.HBM)] * 5,
         out_specs=pl.BlockSpec(memory_space=pltpu.VMEM),
         scratch_shapes=[
+            pltpu.VMEM(taps_x.shape, BF16),
+            pltpu.VMEM(taps_y.shape, BF16),
+            pltpu.VMEM(mix_weight.shape, BF16),
+            pltpu.VMEM((C,), BF16),
             pltpu.VMEM((T, CB, H, W), BF16),
-            pltpu.VMEM((T, cq, FH, FW), BF16),
+            pltpu.VMEM((T, nr, nco, cq, H, W), BF16),
             pltpu.VMEM((cq, FW, FW), BF16),
             pltpu.VMEM((FH * cq, cq * FH), BF16),
             pltpu.VMEM((16 * H, 16 * H), BF16),
@@ -326,7 +358,7 @@
             pltpu.VMEM((T, rp, C, W), BF16),
             pltpu.VMEM((T, rp, C, W), BF16),
             pltpu.VMEM((T, H, CB, W), BF16),
-            pltpu.SemaphoreType.DMA((1 + T,)),
+            pltpu.SemaphoreType.DMA((5 + T,)),
             pltpu.SemaphoreType.DMA,
             pltpu.SemaphoreType.DMA((T,)),
             pltpu.SemaphoreType.DMA,
@@ -337,7 +369,7 @@
         compiler_params=pltpu.CompilerParams(
             collective_id=0, has_side_effects=True, vmem_limit_bytes=40 * 1024 * 1024
         ),
-    )(feature_map, taps_x, taps_y, mix_weight, mix_bias.reshape(1, C))
+    )(*(pltpu.with_memory_space_constraint(v, pltpu.HBM) for v in (feature_map, taps_x, taps_y, mix_weight, mix_bias)))
 
 
 def fits_kernel(mesh):

time: 78.3 us -> 70.5 us (0.900)
  local copies, waits for them, and re-layouts: 5.53 us -> 1.06 us
  Pallas kernels: 72.4 us -> 69.3 us
    unnamed x9 -> x1, local copies, waits for them, and re-layouts: 4.85 us -> 1.06 us
    pallas_call x1, Pallas kernels: 72.4 us -> 69.3 us  [per_device(): pl.pallas_call(functools.partial(section_kernel, dims), out_shape=jax.Sha...]
where the time goes in v2:
time: 70.5 us; the launch traced here: 70.4 us
  Pallas kernels  69.3 us (98%)
  local copies, waits for them, and re-layouts  1.06 us (2%)
    pallas_call x1, Pallas kernels, per_device(): pl.pallas_call(functools.partial(section_kernel, dims), out_shape=jax.Sha...  69.3 us

profile of v2, /device:TPU:0, one launch (start us, length us, event | category | flops | bytes accessed | tf_op | source)
XLA Modules:
  0.0 70.4 jit_solution(11551379908130563433)
XLA Ops:
  0.0 69.3 %shard_map.55 = bf16[5,64,16,128]{3,2,1,0:T(8,128)(2,1)S(1)} custom-call(bf16[5,64,16,128]{3,2,1,0:T(8,128)(2,1)} %feat_hbm.1, bf16[64,63]{1,0:T(8,128)(2,1)} %tapx_hbm.1, bf16[64,63]{1,0:T(8,128)(2,1)} %tapy_hbm.1, bf16[512,512]{1,0:T(8,128)(2,1)} %weight_hbm.1, bf16[512]{0:T(512)(128)(2,1)} %bias_hbm.1), custom_call_target="tpu_custom_call" | custom-call | tf_op jit(solution)/shard_map/pallas_call | solution.py:340
  69.3 1.1 %copy.7 = bf16[5,64,16,128]{3,2,1,0:T(8,128)(2,1)} copy(bf16[5,64,16,128]{3,2,1,0:T(8,128)(2,1)S(1)} %shard_map.55) | data formatting | bytes 2621440

commit v3 on v2

--- a/solution.py
+++ b/solution.py
@@ -160,7 +160,7 @@
                     device_id_type=MESH,
                 ).start()
 
-    ahead = 2
+    ahead = 3
     for t in range(min(ahead, T)):
         share(t, 0, cq)
 
@@ -250,7 +250,7 @@
             def _():
                 share(t + ahead, s * cs, cs)
 
-            i = s + 1
+            i = lax.rem((nch // 2) * (s + 1) - 1, nch - 1) + 1
             for dr in range(nr):
                 for dc in range(nco):
                     push(i, dr, dc)
@@ -303,7 +303,7 @@
                 feat[t, g * 16 : (g + 1) * 16].astype(F32) + branch
             ).astype(BF16)
 
-    lag1, lag2 = 2, 4
+    lag1, lag2 = 3, 5
 
     @pl.loop(0, T + lag2)
     def _(s):

time: 70.5 us -> 70.2 us (level)
  no operation moved by 1% of the time
where the time goes in v3:
time: 70.2 us; the launch traced here: 70.1 us
  Pallas kernels  69 us (98%)
  local copies, waits for them, and re-layouts  1.06 us (2%)
    pallas_call x1, Pallas kernels, per_device(): pl.pallas_call(functools.partial(section_kernel, dims), out_shape=jax.Sha...  69 us

profile of v3, /device:TPU:0, one launch (start us, length us, event | category | flops | bytes accessed | tf_op | source)
XLA Modules:
  0.0 70.1 jit_solution(16457232879468287239)
XLA Ops:
  0.0 69.0 %shard_map.55 = bf16[5,64,16,128]{3,2,1,0:T(8,128)(2,1)S(1)} custom-call(bf16[5,64,16,128]{3,2,1,0:T(8,128)(2,1)} %feat_hbm.1, bf16[64,63]{1,0:T(8,128)(2,1)} %tapx_hbm.1, bf16[64,63]{1,0:T(8,128)(2,1)} %tapy_hbm.1, bf16[512,512]{1,0:T(8,128)(2,1)} %weight_hbm.1, bf16[512]{0:T(512)(128)(2,1)} %bias_hbm.1), custom_call_target="tpu_custom_call" | custom-call | tf_op jit(solution)/shard_map/pallas_call | solution.py:340
  69.0 1.1 %copy.7 = bf16[5,64,16,128]{3,2,1,0:T(8,128)(2,1)} copy(bf16[5,64,16,128]{3,2,1,0:T(8,128)(2,1)S(1)} %shard_map.55) | data formatting | bytes 2621440
